TPU v7x, 32 devices: a whole 2x2x4 slice. The times are simulated.
32 devices in a mesh: inner: 4 (over y, x), outer: 8 (over z, core).
Axes of the slice: x: 2, y: 2, z: 4, core: 2. Of those that a mesh axis runs over, the one named last changes fastest.
Arguments:
- jac: float32 [512, 256, 256], P(('outer', 'inner')), may hold values from -0.5 to 1
- obs: float32 [512, 256], P(('outer', 'inner')), may hold values from -6 to 6
- gain_filter: float32 [256], replicated, may hold values from 0 to 0.1
- gain_smooth: float32 [256, 256], replicated, may hold values from -0.5 to 1
- init_mean: float32 [256], replicated, may hold values from -6 to 6
Outputs:
- filtered: float32 [512, 256], P(('outer', 'inner'))
- smoothed: float32 [512, 256], P(('outer', 'inner'))
All inputs are finite; a program needn't handle non-finite values.
Results may differ from a plain program's by a relative error of at most 0.0003.
Values sent between devices are 32-bit elements; how exact they have to be, the bound alone decides.
A program may use at most 64 MiB of HBM per device.

v0:
```python
import jax
import jax.numpy as jnp
from jax import lax
from jax.sharding import PartitionSpec as P

HIGHEST = lax.Precision.HIGHEST


def entering(part, axis, combine, identity):
    place = lax.axis_index(axis)
    gathered = lax.all_gather(part, axis)
    state = jnp.zeros_like(part) + jnp.asarray(identity, part.dtype)

    def one(turn, state):
        return combine(state, lax.dynamic_index_in_dim(gathered, turn, 0, False))

    return lax.fori_loop(0, place, one, state)


def last_row(state_width):
    return (jnp.arange(state_width + 1) == state_width).astype(jnp.float32)[:, None]


def identity_map(state_width):
    return jnp.concatenate(
        [jnp.eye(state_width, dtype=jnp.float32), jnp.zeros((1, state_width), jnp.float32)], 0
    )


def compose(earlier, later):
    state_width = later.shape[1]
    product = jnp.dot(earlier, later[:state_width], precision=HIGHEST)
    return product + last_row(state_width) * later[state_width][None, :]


def advance(packed, state):
    state_width = packed.shape[1]
    return jnp.dot(state, packed[:state_width], precision=HIGHEST) + packed[state_width]


def raise_power(factor, count):
    result = jnp.eye(factor.shape[0], dtype=jnp.float32)
    square = factor
    while count > 0:
        if count % 2 == 1:
            result = jnp.dot(result, square, precision=HIGHEST)
        count = count // 2
        if count > 0:
            square = jnp.dot(square, square, precision=HIGHEST)
    return result


def incoming_state(own_map, boundary):
    state_width = own_map.shape[1]
    identity = identity_map(state_width)
    inner_count = lax.axis_size("inner")
    inner_here = lax.axis_index("inner")
    gathered = lax.all_gather(own_map[None], "inner", axis=0, tiled=True)

    def absorb(running, inputs):
        before, group_total = running
        segment, position = inputs
        group_total = compose(group_total, segment)
        taken = position < inner_here
        before = jnp.where(taken, group_total, before)
        return ((before, group_total), None)

    (seg_before, group_total), _ = lax.scan(
        absorb,
        (identity, identity),
        (gathered, jnp.arange(inner_count, dtype=jnp.int32)),
        reverse=False,
    )
    group_before = entering(group_total, "outer", compose, identity)
    group_state = advance(group_before, boundary)
    return advance(seg_before, group_state)


def entering_backward(offset_sum, step_power):
    inner_count = lax.axis_size("inner")
    inner_here = lax.axis_index("inner")
    outer_count = lax.axis_size("outer")
    outer_here = lax.axis_index("outer")
    zero_state = jnp.zeros_like(offset_sum)
    seg_offsets = lax.all_gather(offset_sum[None], "inner", axis=0, tiled=True)

    def run_affine(power, here):

        def turn(running, inputs):
            state, caught = running
            offset, position = inputs
            caught = jnp.where(position == here, state, caught)
            state = jnp.dot(state, power, precision=HIGHEST) + offset
            return ((state, caught), None)

        return turn

    (group_offset, _), _ = lax.scan(
        run_affine(step_power, inner_here),
        (zero_state, zero_state),
        (seg_offsets, jnp.arange(inner_count, dtype=jnp.int32)),
        reverse=True,
    )
    group_power = raise_power(step_power, inner_count)
    group_offsets = lax.all_gather(group_offset[None], "outer", axis=0, tiled=True)
    (_, group_state), _ = lax.scan(
        run_affine(group_power, outer_here),
        (zero_state, zero_state),
        (group_offsets, jnp.arange(outer_count, dtype=jnp.int32)),
        reverse=True,
    )
    (_, device_state), _ = lax.scan(
        run_affine(step_power, inner_here),
        (group_state, group_state),
        (seg_offsets, jnp.arange(inner_count, dtype=jnp.int32)),
        reverse=True,
    )
    return device_state


def shards(jac, obs, gain_filter, gain_smooth, init_mean):
    state_width = jac.shape[1]
    step_count = jac.shape[0]
    retain = 1.0 - gain_filter
    bottom = last_row(state_width)

    def compose_forward(packed, inputs):
        step_matrix, measured = inputs
        moved = (
            lax.dot_general(packed, step_matrix, (((1,), (1,)), ((), ())), precision=HIGHEST)
            * retain[None, :]
        )
        return (moved + bottom * (gain_filter * measured)[None, :], None)

    forward_map, _ = lax.scan(compose_forward, identity_map(state_width), (jac, obs))
    start_state = incoming_state(forward_map, init_mean)

    def forward(state, inputs):
        step_matrix, measured = inputs
        predicted = jnp.dot(step_matrix, state, precision=HIGHEST)
        updated = predicted + gain_filter * (measured - predicted)
        return (updated, (predicted, updated))

    _, (predicted_all, filtered_all) = lax.scan(forward, start_state, (jac, obs))
    correction = filtered_all - predicted_all

    def backward(state, term):
        renewed = jnp.dot(gain_smooth, state, precision=HIGHEST) + term
        return (renewed, renewed)

    zero_state = jnp.zeros((state_width,), jnp.float32)
    offset_sum, _ = lax.scan(backward, zero_state, correction, reverse=True)
    step_power = raise_power(gain_smooth.T, step_count)
    after_state = entering_backward(offset_sum, step_power)
    _, back_states = lax.scan(backward, after_state, correction, reverse=True)
    return (filtered_all, predicted_all + back_states)


def solution(mesh):
    return jax.shard_map(
        shards,
        mesh=mesh,
        in_specs=(P(("outer", "inner"), None, None), P(("outer", "inner"), None), P(), P(), P()),
        out_specs=(P(("outer", "inner"), None), P(("outer", "inner"), None)),
        check_vma=False,
    )
```

profile of v0, /device:TPU:0, one launch (start us, length us, event | category | flops | bytes accessed | tf_op | source)
XLA Modules:
  0.0 221.8 jit_solution(6826046817942252627)
XLA Ops:
  8.0 34.7 %while.131 = (s32[]{:T(128)}, f32[257,256]{1,0:T(8,128)S(1)}, f32[16,256,256]{2,1,0:T(8,128)}, f32[256]{0:T(256)S(1)}, f32[256]{0:T(256)}, /*index=5*/f32[16,256]{1,0:T(8,128)}, s32[]{:T(128)}) while((s32[]{:T(128)}, f32[257,256]{1,0:T(8,128)S(1)}, f32[16,256,256]{2,1,0:T(8,128)}, f32[256]{0:T(256)S(1)}, f32[256]{0:T(256)}, ...), condition=%wide.region_1.2_spmd.clone, body=%wide.region_0.1_spmd.clone.sunk | while | flops 202311168 | bytes 1322585 | solution.py:135
  8.8 1.4 fusion.109
  10.9 1.4 fusion.109
  13.1 1.4 fusion.109
  15.3 1.4 fusion.109
  17.4 1.4 fusion.109
  19.6 1.4 fusion.109
  21.8 1.4 fusion.109
  23.9 1.4 fusion.109
  26.1 1.4 fusion.109
  28.3 1.4 fusion.109
  30.5 1.4 fusion.109
  32.6 1.4 fusion.109
  34.8 1.4 fusion.109
  37.0 1.4 fusion.109
  39.1 1.4 fusion.109
  41.3 1.4 fusion.109
  43.5 29.5 %all-gather.11.cloned.1.call-done = f32[4,257,256]{2,1,0:T(8,128)} async-done(((f32[1,257,256]{2,1,0:T(8,128)}), f32[4,257,256]{2,1,0:T(8,128)}) %all-gather.11.cloned.1.call-update) | async-done | bytes 1052688 | tf_op jit(solution)/shard_map/all_gather | solution.py:58
  73.1 14.0 %while.126 = (s32[]{:T(128)}, f32[257,256]{1,0:T(8,128)S(1)}, f32[257,256]{1,0:T(8,128)S(1)}, s32[4]{0:T(128)S(1)}, s32[]{:T(128)}, /*index=5*/f32[4,257,256]{2,1,0:T(8,128)}, s32[]{:T(128)}, s32[]{:T(128)}, s32[]{}) while((s32[]{:T(128)}, f32[257,256]{1,0:T(8,128)S(1)}, f32[257,256]{1,0:T(8,128)S(1)}, s32[4]{0:T(128)S(1)}, s32[]{:T(128)}, ...), condition=%wide.region_3.4_spmd, body=%wide.region_2.3_spmd.sunk | while | flops 202310912 | bytes 1846927 | solution.py:68
  75.1 1.5 broadcast_select_fusion.9
  78.6 1.5 broadcast_select_fusion.9
  82.1 1.5 broadcast_select_fusion.9
  85.6 1.5 broadcast_select_fusion.9
  91.0 26.7 %all-gather.13.cloned.1.call-done = f32[8,257,256]{2,1,0:T(8,128)} async-done(((f32[1,257,256]{2,1,0:T(8,128)}), f32[8,257,256]{2,1,0:T(8,128)}) %all-gather.13.cloned.1.call-update) | async-done | bytes 2105360 | tf_op jit(solution)/shard_map/all_gather | solution.py:11
  118.3 33.3 %while.128 = (s32[]{:T(128)}, f32[256]{0:T(256)S(1)}, f32[16,256]{1,0:T(8,128)S(1)}, f32[16,256]{1,0:T(8,128)S(1)}, f32[16,256,256]{2,1,0:T(8,128)}, /*index=5*/...) while((s32[]{:T(128)}, f32[256]{0:T(256)S(1)}, f32[16,256]{1,0:T(8,128)S(1)}, ...), condition=%wide.region_7.8_spmd, body=%wide.region_6.7_spmd.sunk | while | flops 787202 | bytes 275049 | solution.py:144
  118.3 1.2 fusion.99
  119.5 0.8 constant_dynamic-slice_fusion.18
  120.4 1.2 fusion.99
  121.6 0.8 constant_dynamic-slice_fusion.18
  122.5 1.2 fusion.99
  123.7 0.8 constant_dynamic-slice_fusion.18
  124.6 1.2 fusion.99
  125.8 0.8 constant_dynamic-slice_fusion.18
  126.6 1.2 fusion.99
  127.9 0.8 constant_dynamic-slice_fusion.18
  128.7 1.2 fusion.99
  129.9 0.8 constant_dynamic-slice_fusion.18
  130.8 1.2 fusion.99
  132.0 0.8 constant_dynamic-slice_fusion.18
  132.9 1.2 fusion.99
  134.1 0.8 constant_dynamic-slice_fusion.18
  135.0 1.2 fusion.99
  136.2 0.8 constant_dynamic-slice_fusion.18
  137.1 1.2 fusion.99
  138.3 0.8 constant_dynamic-slice_fusion.18
  139.1 1.2 fusion.99
  140.4 0.8 constant_dynamic-slice_fusion.18
  141.2 1.2 fusion.99
  142.4 0.8 constant_dynamic-slice_fusion.18
  143.3 1.2 fusion.99
  144.5 0.8 constant_dynamic-slice_fusion.18
  145.4 1.2 fusion.99
  146.6 0.8 constant_dynamic-slice_fusion.18
  147.5 1.2 fusion.99
  148.7 0.8 constant_dynamic-slice_fusion.18
  149.5 1.2 fusion.99
  150.8 0.8 constant_dynamic-slice_fusion.18
  151.6 6.1 %while.132 = (s32[]{:T(128)}, f32[256]{0:T(256)S(1)}, f32[256,256]{1,0:T(8,128)S(1)}, f32[16,256]{1,0:T(8,128)S(1)}, s32[]{:T(128)}, /*index=5*/s32[]{:T(128)}, s32[]{:T(128)}) while((s32[]{:T(128)}, f32[256]{0:T(256)S(1)}, f32[256,256]{1,0:T(8,128)S(1)}, f32[16,256]{1,0:T(8,128)S(1)}, s32[]{:T(128)}, /*index=5*/s32[]{:T(128)}, ...), condition=%wide.region_9.10_spmd.clone, body=%wide.region_8.9_spmd.clone.sunk | while | flops 786948 | bytes 271463 | solution.py:152
  157.7 8.0 %all-gather.6 = f32[4,1,256]{2,1,0:T(1,128)S(1)} all-gather(f32[1,1,256]{2,1,0:T(1,128)S(1)} %bitcast.222), channel_id=4, replica_groups=mesh['inner'=4,'outer'=8] {'inner'}, dimensions={0}, use_global_device_ids=true | all-gather | bytes 5120 | tf_op jit(solution)/shard_map/all_gather | solution.py:85
  165.8 1.1 while.133
  166.9 22.8 %all-gather.7 = f32[8,1,256]{2,1,0:T(1,128)S(1)} all-gather(f32[1,1,256]{2,1,0:T(1,128)S(1)} %bitcast.221), channel_id=5, replica_groups=mesh['inner'=4,'outer'=8] {'outer'}, dimensions={0}, use_global_device_ids=true | all-gather | bytes 9216 | tf_op jit(solution)/shard_map/all_gather | solution.py:105
  189.7 12.2 %while.134 = (s32[]{:T(128)}, f32[256]{0:T(256)S(1)}, f32[256]{0:T(256)S(1)}, f32[256,256]{1,0:T(8,128)S(1)}, f32[8,256]{1,0:T(8,128)S(1)}, /*index=5*/s32[8]{0:...) while((s32[]{:T(128)}, f32[256]{0:T(256)S(1)}, f32[256]{0:T(256)S(1)}, ...), condition=%wide.region_13.14_spmd.clone, body=%wide.region_12.13_spmd.clone.sunk | while | flops 787461 | bytes 273557 | solution.py:106
  201.9 6.0 %while.129 = (s32[]{:T(128)}, f32[256]{0:T(256)S(1)}, f32[256]{0:T(256)S(1)}, f32[256,256]{1,0:T(8,128)S(1)}, f32[4,256]{1,0:T(4,128)S(1)}, /*index=5*/s32[4]{0:T(128)S(1)}, s32[]{:T(128)}, s32[]{:T(128)}, s32[]{:T(128)}) while((s32[]{:T(128)}, f32[256]{0:T(256)S(1)}, f32[256]{0:T(256)S(1)}, f32[256,256]{1,0:T(8,128)S(1)}, ...), condition=%wide.region_15.16_spmd, body=%wide.region_14.15_spmd.sunk | while | flops 786948 | bytes 272515 | solution.py:112
  207.9 6.3 %while.130 = (s32[]{:T(128)}, f32[256]{0:T(256)S(1)}, f32[16,256]{1,0:T(8,128)S(1)}, f32[256,256]{1,0:T(8,128)S(1)}, f32[16,256]{1,0:T(8,128)S(1)}, /*index=5*/s32[]{:T(128)}, s32[]{:T(128)}, s32[]{:T(128)}) while((s32[]{:T(128)}, f32[256]{0:T(256)S(1)}, f32[16,256]{1,0:T(8,128)S(1)}, f32[256,256]{1,0:T(8,128)S(1)}, ...), condition=%wide.region_17.18_spmd, body=%wide.region_16.17_spmd.sunk | while | flops 786691 | bytes 271465 | solution.py:155
  (368 shorter events, 47.7 us)
Async XLA Ops:
  7.2 110.5 %copy-start = (f32[256]{0:T(256)S(1)}, f32[256]{0:T(256)}, u32[]{:S(2)}) copy-start(f32[256]{0:T(256)} %param.27) | copy-start | bytes 3076
  7.2 65.9 %all-gather.11.cloned.1.call-start = ((), (), s32[]{:S(2)}) async-start(), calls=%async_computation | async-start | bytes 1351680 | tf_op jit(solution)/shard_map/all_gather | solution.py:58
  42.7 0.7 copy-start.3
  43.4 74.2 %all-gather.13.cloned.1.call-start = ((), (), s32[]{:S(2)}) async-start(), calls=%async_computation.1 | async-start | bytes 2433024 | tf_op jit(solution)/shard_map/all_gather | solution.py:11
  73.1 14.8 %copy-start.1 = (f32[256,256]{1,0:T(8,128)S(1)}, f32[256,256]{1,0:T(8,128)}, u32[]{:S(2)}) copy-start(f32[256,256]{1,0:T(8,128)} %param.26) | copy-start | bytes 786436
  87.1 0.7 copy-start.2
  117.6 0.7 copy-start.4
  151.6 38.1 %copy-start.5 = (f32[16,256]{1,0:T(8,128)}, f32[16,256]{1,0:T(8,128)S(1)}, u32[]{:S(2)}) copy-start(f32[16,256]{1,0:T(8,128)S(1)} %get-tuple-element.684) | copy-start | bytes 49156
Sparse Core Ops, SparseCore 0:
  43.5 29.4 all-gather.10
  87.9 29.6 all-gather.12
where the time goes:
time: 225 us; the launch traced here: 222 us
  matrix products  62.5 us (28%)
  waiting for transfers between devices  56.2 us (25%)
  blocking collectives  30.9 us (14%)
  local copies, waits for them, and re-layouts  30.6 us (14%)
  between operations  14.4 us (6%)
  other arithmetic  14.1 us (6%)
  loops' own time  13 us (6%)
    all_gather x1, waiting for transfers between devices, incoming_state(): gathered = lax.all_gather(own_map[None], 'inner', axis=0, tiled=True)  29.5 us
    all_gather x1, waiting for transfers between devices, entering(): gathered = lax.all_gather(part, axis)  26.7 us
    all_gather x1, blocking collectives, entering_backward(): lax.all_gather(group_offset[None], 'outer', axis=0, tiled=True)  22.8 us
    dot_general x16, matrix products, compose_forward(): lax.dot_general(packed, step_matrix, (((1,), (1,)), ((), ())), precision=...  21.9 us
    dot_general x16, matrix products, forward(): predicted = jnp.dot(step_matrix, state, precision=HIGHEST)  19.5 us
    dynamic_slice x48, local copies, waits for them, and re-layouts, shards(): lax.scan(compose_forward, identity_map(state_width), (jac, obs))  13.3 us
    mul x16, other arithmetic, compose_forward(): return (moved + bottom * (gain_filter * measured)[None, :], None)  11.6 us
    dot_general x32, matrix products, backward(): renewed = jnp.dot(gain_smooth, state, precision=HIGHEST) + term  8.65 us
  transfers between devices with their start and end apart: 2, of which 2 were waited for; matrix products, arithmetic and copies ran while one was open for 1% of the time, Pallas kernels for 0%

commit v1 on v0

--- a/solution.py
+++ b/solution.py
@@ -55,7 +55,14 @@
     identity = identity_map(state_width)
     inner_count = lax.axis_size("inner")
     inner_here = lax.axis_index("inner")
-    gathered = lax.all_gather(own_map[None], "inner", axis=0, tiled=True)
+    ways, here_2 = (lax.axis_size("inner"), lax.axis_index("inner"))
+    gathered, reach = (own_map[None], 1)
+    while reach < ways:
+        theirs = lax.ppermute(gathered, "inner", [(d, d ^ reach) for d in range(ways)])
+        mine_first = jnp.concatenate([gathered, theirs], axis=0)
+        theirs_first = jnp.concatenate([theirs, gathered], axis=0)
+        gathered = jnp.where(here_2 & reach == 0, mine_first, theirs_first)
+        reach = 2 * reach
 
     def absorb(running, inputs):
         before, group_total = running

time: 225 us -> 214 us (0.951)
  waiting for transfers between devices: 56.2 us -> 45.5 us
  starting transfers between devices: 0.08 us -> 4.9 us
  matrix products: 62.5 us -> 58.7 us
  local copies, waits for them, and re-layouts: 30.6 us -> 28.2 us
    all_gather x1 -> x0, waiting for transfers between devices: 29.5 us -> none  [incoming_state(): gathered = lax.all_gather(own_map[None], 'inner', axis=0, tiled=True)]
    ppermute x0 -> x2, waiting for transfers between devices: none -> 17.6 us  [incoming_state(): lax.ppermute(gathered, 'inner', [(d, d ^ reach) for d in range(ways)])]
    ppermute x0 -> x2, starting transfers between devices: none -> 4.86 us  [incoming_state(): lax.ppermute(gathered, 'inner', [(d, d ^ reach) for d in range(ways)])]
    dot_general x4, matrix products: 5.96 us -> 2.2 us  [compose(): product = jnp.dot(earlier, later[:state_width], precision=HIGHEST)]
    slice x4, local copies, waits for them, and re-layouts: 2.85 us -> 0.04 us  [compose(): return product + last_row(state_width) * later[state_width][None, :]]
  transfers between devices with their start and end apart: 2 -> 3, of which waited for: 2 -> 3; matrix products, arithmetic and copies ran while one was open for 1% -> 1% of each run, Pallas kernels for 0% -> 0%
where the time goes in v1:
time: 214 us; the launch traced here: 211 us
  matrix products  58.7 us (27%)
  waiting for transfers between devices  45.5 us (21%)
  blocking collectives  30.9 us (14%)
  local copies, waits for them, and re-layouts  28.2 us (13%)
  other arithmetic  15.6 us (7%)
  between operations  14.4 us (7%)
  loops' own time  13.1 us (6%)
  starting transfers between devices  4.9 us (2%)
    all_gather x1, waiting for transfers between devices, entering(): gathered = lax.all_gather(part, axis)  27.9 us
    all_gather x1, blocking collectives, entering_backward(): lax.all_gather(group_offset[None], 'outer', axis=0, tiled=True)  22.8 us
    dot_general x16, matrix products, compose_forward(): lax.dot_general(packed, step_matrix, (((1,), (1,)), ((), ())), precision=...  21.9 us
    dot_general x16, matrix products, forward(): predicted = jnp.dot(step_matrix, state, precision=HIGHEST)  19.5 us
    ppermute x2, waiting for transfers between devices, incoming_state(): lax.ppermute(gathered, 'inner', [(d, d ^ reach) for d in range(ways)])  17.6 us
    dynamic_slice x48, local copies, waits for them, and re-layouts, shards(): lax.scan(compose_forward, identity_map(state_width), (jac, obs))  13.3 us
    mul x16, other arithmetic, compose_forward(): return (moved + bottom * (gain_filter * measured)[None, :], None)  11.6 us
    dot_general x32, matrix products, backward(): renewed = jnp.dot(gain_smooth, state, precision=HIGHEST) + term  8.65 us
  transfers between devices with their start and end apart: 3, of which 3 were waited for; matrix products, arithmetic and copies ran while one was open for 1% of the time, Pallas kernels for 0%

profile of v1, /device:TPU:0, one launch (start us, length us, event | category | flops | bytes accessed | tf_op | source)
XLA Modules:
  0.0 211.4 jit_solution(3441077741526511450)
XLA Ops:
  8.0 34.6 %while.131 = (s32[]{:T(128)}, f32[257,256]{1,0:T(8,128)S(1)}, f32[16,256,256]{2,1,0:T(8,128)}, f32[256]{0:T(256)S(1)}, f32[256]{0:T(256)}, /*index=5*/f32[16,256]{1,0:T(8,128)}, s32[]{:T(128)}) while((s32[]{:T(128)}, f32[257,256]{1,0:T(8,128)S(1)}, f32[16,256,256]{2,1,0:T(8,128)}, f32[256]{0:T(256)S(1)}, f32[256]{0:T(256)}, ...), condition=%wide.region_1.2_spmd.clone, body=%wide.region_0.1_spmd.clone.sunk | while | flops 202311168 | bytes 1322585 | solution.py:142
  8.8 1.4 fusion.108
  11.0 1.4 fusion.108
  13.1 1.4 fusion.108
  15.3 1.4 fusion.108
  17.5 1.4 fusion.108
  19.6 1.4 fusion.108
  21.8 1.4 fusion.108
  24.0 1.4 fusion.108
  26.1 1.4 fusion.108
  28.3 1.4 fusion.108
  30.5 1.4 fusion.108
  32.6 1.4 fusion.108
  34.8 1.4 fusion.108
  37.0 1.4 fusion.108
  39.1 1.4 fusion.108
  41.3 1.4 fusion.108
  42.9 3.0 %collective-permute-start = (f32[1,257,256]{2,0,1:T(1,128)S(1)}, f32[1,257,256]{2,0,1:T(1,128)S(1)}, u32[]{:S(2)}, u32[]{:S(2)}) collective-permute-start(f32[1,257,256]{2,0,1:T(1,128)S(1)} %broadcast_in_dim.30), channel_id=1, source_target_pairs={{0,8},{8,0},{16,24},{24,16},{1,9},{9,1},{17,25},{25,17},{2,10},{10... | collective-permute-start | bytes 789512 | tf_op jit(solution)/shard_map/ppermute | solution.py:61
  45.9 6.3 %collective-permute-done = f32[1,257,256]{2,0,1:T(1,128)S(1)} collective-permute-done((f32[1,257,256]{2,0,1:T(1,128)S(1)}, f32[1,257,256]{2,0,1:T(1,128)S(1)}, u32[]{:S(2)}, u32[]{:S(2)}) %collective-permute-start) | collective-permute-done | bytes 263200 | tf_op jit(solution)/shard_map/ppermute | solution.py:61
  52.2 0.8 maximum_select_fusion.1
  53.0 1.8 collective-permute-start.1
  54.9 11.3 %collective-permute-done.1 = f32[2,257,256]{2,0,1:T(2,128)S(1)} collective-permute-done((f32[2,257,256]{2,0,1:T(2,128)S(1)}, f32[2,257,256]{2,0,1:T(2,128)S(1)}, u32[]{:S(2)}, u32[]{:S(2)}) %collective-permute-start.1) | collective-permute-done | bytes 526368 | tf_op jit(solution)/shard_map/ppermute | solution.py:61
  67.0 8.4 %while.126 = (s32[]{:T(128)}, f32[257,256]{1,0:T(8,128)S(1)}, f32[257,256]{1,0:T(8,128)S(1)}, s32[4]{0:T(128)S(1)}, s32[]{:T(128)}, /*index=5*/f32[4,257,256]{2,0,1:T(4,128)S(1)}, s32[]{:T(128)}, s32[]{:T(128)}, s32[]{}) while((s32[]{:T(128)}, f32[257,256]{1,0:T(8,128)S(1)}, f32[257,256]{1,0:T(8,128)S(1)}, s32[4]{0:T(128)S(1)}, s32[]{:T(128)}, ...), condition=%wide.region_3.4_spmd, body=%wide.region_2.3_spmd.sunk | while | flops 202310912 | bytes 2370707 | solution.py:75
  79.4 27.9 %all-gather.8.cloned.1.call-done = f32[8,257,256]{2,1,0:T(8,128)} async-done(((f32[1,257,256]{2,1,0:T(8,128)}), f32[8,257,256]{2,1,0:T(8,128)}) %all-gather.8.cloned.1.call-update) | async-done | bytes 2105360 | tf_op jit(solution)/shard_map/all_gather | solution.py:11
  107.9 33.3 %while.128 = (s32[]{:T(128)}, f32[256]{0:T(256)S(1)}, f32[16,256]{1,0:T(8,128)S(1)}, f32[16,256]{1,0:T(8,128)S(1)}, f32[16,256,256]{2,1,0:T(8,128)}, /*index=5*/...) while((s32[]{:T(128)}, f32[256]{0:T(256)S(1)}, f32[16,256]{1,0:T(8,128)S(1)}, ...), condition=%wide.region_7.8_spmd, body=%wide.region_6.7_spmd.sunk | while | flops 787202 | bytes 275049 | solution.py:151
  107.9 1.2 fusion.98
  109.1 0.8 constant_dynamic-slice_fusion.21
  110.0 1.2 fusion.98
  111.2 0.8 constant_dynamic-slice_fusion.21
  112.1 1.2 fusion.98
  113.3 0.8 constant_dynamic-slice_fusion.21
  114.2 1.2 fusion.98
  115.4 0.8 constant_dynamic-slice_fusion.21
  116.2 1.2 fusion.98
  117.5 0.8 constant_dynamic-slice_fusion.21
  118.3 1.2 fusion.98
  119.5 0.8 constant_dynamic-slice_fusion.21
  120.4 1.2 fusion.98
  121.6 0.8 constant_dynamic-slice_fusion.21
  122.5 1.2 fusion.98
  123.7 0.8 constant_dynamic-slice_fusion.21
  124.6 1.2 fusion.98
  125.8 0.8 constant_dynamic-slice_fusion.21
  126.6 1.2 fusion.98
  127.9 0.8 constant_dynamic-slice_fusion.21
  128.7 1.2 fusion.98
  129.9 0.8 constant_dynamic-slice_fusion.21
  130.8 1.2 fusion.98
  132.0 0.8 constant_dynamic-slice_fusion.21
  132.9 1.2 fusion.98
  134.1 0.8 constant_dynamic-slice_fusion.21
  135.0 1.2 fusion.98
  136.2 0.8 constant_dynamic-slice_fusion.21
  137.1 1.2 fusion.98
  138.3 0.8 constant_dynamic-slice_fusion.21
  139.1 1.2 fusion.98
  140.4 0.8 constant_dynamic-slice_fusion.21
  141.2 6.1 %while.132 = (s32[]{:T(128)}, f32[256]{0:T(256)S(1)}, f32[256,256]{1,0:T(8,128)S(1)}, f32[16,256]{1,0:T(8,128)S(1)}, s32[]{:T(128)}, /*index=5*/s32[]{:T(128)}, s32[]{:T(128)}) while((s32[]{:T(128)}, f32[256]{0:T(256)S(1)}, f32[256,256]{1,0:T(8,128)S(1)}, f32[16,256]{1,0:T(8,128)S(1)}, s32[]{:T(128)}, /*index=5*/s32[]{:T(128)}, ...), condition=%wide.region_9.10_spmd.clone, body=%wide.region_8.9_spmd.clone.sunk | while | flops 786948 | bytes 271463 | solution.py:159
  147.3 8.0 %all-gather.4 = f32[4,1,256]{2,1,0:T(1,128)S(1)} all-gather(f32[1,1,256]{2,1,0:T(1,128)S(1)} %bitcast.222), channel_id=3, replica_groups=mesh['inner'=4,'outer'=8] {'inner'}, dimensions={0}, use_global_device_ids=true | all-gather | bytes 5120 | tf_op jit(solution)/shard_map/all_gather | solution.py:92
  155.4 1.1 while.133
  156.5 22.8 %all-gather.5 = f32[8,1,256]{2,1,0:T(1,128)S(1)} all-gather(f32[1,1,256]{2,1,0:T(1,128)S(1)} %bitcast.221), channel_id=4, replica_groups=mesh['inner'=4,'outer'=8] {'outer'}, dimensions={0}, use_global_device_ids=true | all-gather | bytes 9216 | tf_op jit(solution)/shard_map/all_gather | solution.py:112
  179.3 12.2 %while.134 = (s32[]{:T(128)}, f32[256]{0:T(256)S(1)}, f32[256]{0:T(256)S(1)}, f32[256,256]{1,0:T(8,128)S(1)}, f32[8,256]{1,0:T(8,128)S(1)}, /*index=5*/s32[8]{0:...) while((s32[]{:T(128)}, f32[256]{0:T(256)S(1)}, f32[256]{0:T(256)S(1)}, ...), condition=%wide.region_13.14_spmd.clone, body=%wide.region_12.13_spmd.clone.sunk | while | flops 787461 | bytes 273557 | solution.py:113
  191.5 6.0 %while.129 = (s32[]{:T(128)}, f32[256]{0:T(256)S(1)}, f32[256]{0:T(256)S(1)}, f32[256,256]{1,0:T(8,128)S(1)}, f32[4,256]{1,0:T(4,128)S(1)}, /*index=5*/s32[4]{0:T(128)S(1)}, s32[]{:T(128)}, s32[]{:T(128)}, s32[]{:T(128)}) while((s32[]{:T(128)}, f32[256]{0:T(256)S(1)}, f32[256]{0:T(256)S(1)}, f32[256,256]{1,0:T(8,128)S(1)}, ...), condition=%wide.region_15.16_spmd, body=%wide.region_14.15_spmd.sunk | while | flops 786948 | bytes 272515 | solution.py:119
  197.5 6.4 %while.130 = (s32[]{:T(128)}, f32[256]{0:T(256)S(1)}, f32[16,256]{1,0:T(8,128)S(1)}, f32[256,256]{1,0:T(8,128)S(1)}, f32[16,256]{1,0:T(8,128)S(1)}, /*index=5*/s32[]{:T(128)}, s32[]{:T(128)}, s32[]{:T(128)}) while((s32[]{:T(128)}, f32[256]{0:T(256)S(1)}, f32[16,256]{1,0:T(8,128)S(1)}, f32[256,256]{1,0:T(8,128)S(1)}, ...), condition=%wide.region_17.18_spmd, body=%wide.region_16.17_spmd.sunk | while | flops 786691 | bytes 271465 | solution.py:162
  (379 shorter events, 48.2 us)
Async XLA Ops:
  7.2 100.1 %copy-start = (f32[256]{0:T(256)S(1)}, f32[256]{0:T(256)}, u32[]{:S(2)}) copy-start(f32[256]{0:T(256)} %param.27) | copy-start | bytes 3076
  7.2 100.0 %all-gather.8.cloned.1.call-start = ((), (), s32[]{:S(2)}) async-start(), calls=%async_computation | async-start | bytes 2433024 | tf_op jit(solution)/shard_map/all_gather | solution.py:11
  7.3 47.6 %copy-start.2 = (f32[257,256]{1,0:T(8,128)}, f32[257,256]{1,0:T(8,128)S(1)}, u32[]{:S(2)}) copy-start(f32[257,256]{1,0:T(8,128)S(1)} %pad_convert_fusion) | copy-start | bytes 789508
  42.9 9.4 %collective-permute-start = (f32[1,257,256]{2,0,1:T(1,128)S(1)}, f32[1,257,256]{2,0,1:T(1,128)S(1)}, u32[]{:S(2)}, u32[]{:S(2)}) collective-permute-start(f32[1,257,256]{2,0,1:T(1,128)S(1)} %broadcast_in_dim.30), channel_id=1, source_target_pairs={{0,8},{8,0},{16,24},{24,16},{1,9},{9,1},{17,25},{25,17},{2,10},{10... | collective-permute-start | bytes 789512 | tf_op jit(solution)/shard_map/ppermute | solution.py:61
  53.0 13.2 %collective-permute-start.1 = (f32[2,257,256]{2,0,1:T(2,128)S(1)}, f32[2,257,256]{2,0,1:T(2,128)S(1)}, u32[]{:S(2)}, u32[]{:S(2)}) collective-permute-start(f32[2,257,256]{2,0,1:T(2,128)S(1)} %maximum_select_fusion.1), channel_id=1, source_target_pairs={{0,16},{8,24},{16,0},{24,8},{1,17},{9,25},{17,1},{25,9},{2,18},{10... | collective-permute-start | bytes 1579016 | tf_op jit(solution)/shard_map/ppermute | solution.py:61
  54.9 12.1 %copy-start.5 = (f32[257,256]{1,0:T(8,128)S(1)}, f32[257,256]{1,0:T(8,128)}, u32[]{:S(2)}) copy-start(f32[257,256]{1,0:T(8,128)} %copy-done.2) | copy-start | bytes 789508
  67.0 9.2 %copy-start.1 = (f32[256,256]{1,0:T(8,128)S(1)}, f32[256,256]{1,0:T(8,128)}, u32[]{:S(2)}) copy-start(f32[256,256]{1,0:T(8,128)} %param.26) | copy-start | bytes 786436
  75.4 0.7 copy-start.4
  78.3 29.0 %copy-start.3 = (f32[257,256]{1,0:T(8,128)S(1)}, f32[257,256]{1,0:T(8,128)}, u32[]{:S(2)}) copy-start(f32[257,256]{1,0:T(8,128)} %copy-done.2) | copy-start | bytes 789508
  107.2 0.7 copy-start.6
  141.2 14.1 %copy-start.7 = (f32[16,256]{1,0:T(8,128)}, f32[16,256]{1,0:T(8,128)S(1)}, u32[]{:S(2)}) copy-start(f32[16,256]{1,0:T(8,128)S(1)} %get-tuple-element.684) | copy-start | bytes 49156
Sparse Core Ops, SparseCore 0:
  76.3 30.9 all-gather.7
